TPU v7x, 32 devices: a whole 2x2x4 slice. The times are simulated.
32 devices in a mesh: dp: 2 (over x), seq: 4 (over z), tensor: 4 (over y, core).
Axes of the slice: x: 2, y: 2, z: 4, core: 2. Of those that a mesh axis runs over, the one named last changes fastest.
Arguments:
- tokens: bfloat16 [2, 4, 1024, 768], P('dp', 'seq'), may hold values from -6 to 6
- branch: int32 [2, 4], P('dp', 'seq'), may hold values from 1024 to 2048, as said below
- w_attn: bfloat16 [3, 768, 768], P(None, None, 'tensor'), may hold values from -0.3125 to 0.3125
- w_proj: bfloat16 [768, 768], P('tensor'), may hold values from -6 to 6
- w_expand: bfloat16 [768, 3072], P(None, 'tensor'), may hold values from -0.21875 to 0.21875
- w_contract: bfloat16 [3072, 768], P('tensor'), may hold values from -0.4375 to 0.4375
- attn_bias: float32 [2, 768], P(None, 'tensor'), may hold values from -3 to 3
- branch_bias: float32 [2, 768], replicated, may hold values from -4 to 4
- expand_bias: float32 [3072], P('tensor'), may hold values from -3 to 3
- norm_gains: float32 [2, 768], replicated, may hold values from 0.5 to 1.5
- norm_shifts: float32 [2, 768], replicated, may hold values from -3 to 3
- cotangent: bfloat16 [2, 4, 1024, 768], P('dp', 'seq'), may hold values from -6 to 6
Outputs:
- layer_out: bfloat16 [2, 4, 1024, 768], P('dp', 'seq', 'tensor')
- grad_tokens: bfloat16 [2, 4, 1024, 768], P('dp', 'seq', 'tensor')
- grad_attn: float32 [3, 768, 768], P(None, ('dp', 'seq'), 'tensor')
- grad_proj: float32 [768, 768], P('tensor', ('dp', 'seq'))
- grad_expand: float32 [768, 3072], P(('dp', 'seq'), 'tensor')
- grad_contract: float32 [3072, 768], P('tensor', ('dp', 'seq'))
- grad_attn_bias: float32 [2, 768], P(None, 'tensor')
- grad_branch_bias: float32 [2, 768], replicated
- grad_expand_bias: float32 [3072], P('tensor')
- grad_norm_gains: float32 [2, 768], replicated
- grad_norm_shifts: float32 [2, 768], replicated
Inputs may be any that keep to these rules, and one draw needn't show every extreme that they name: branch[g, 0] equals 2048 in every group: the first continuation sees the whole prompt.
All inputs are finite; a program needn't handle non-finite values.
Results may differ from a plain program's by a relative error of at most 0.013.
The roundings to bfloat16 on the way count: a program that leaves them out, or rounds other values in their place, can miss the bound.
Values may be sent and summed in bfloat16 or wider, within the bound.
A program may use at most 192 MiB of HBM per device.

v0:
```python
import math
import jax
import jax.numpy as jnp
from jax import lax
from jax.sharding import PartitionSpec as P

HEAD_DIM = 64
LAYERS = 12
PCH = 512
CLEN = 512
norm_eps = 1e-05
big_negative = -1000000000.0


def layer_norm(value, gain, shift):
    centre = jnp.mean(value, axis=-1, keepdims=True)
    centred = value - centre
    spread = jnp.mean(centred * centred, axis=-1, keepdims=True)
    return centred * lax.rsqrt(spread + norm_eps) * gain + shift


def scores_of(queries, all_keys, allowed, score_scale):
    raw = (
        jnp.einsum("ihd,jhd->hij", queries, all_keys, preferred_element_type=jnp.float32)
        * score_scale
    )
    return jnp.where(allowed[None], raw, big_negative)


def attend(queries, all_keys, all_values, allowed, score_scale):
    scores = scores_of(queries, all_keys, allowed, score_scale)
    highest_score = jnp.max(scores, axis=-1, keepdims=True)
    exponent = jnp.exp(scores - highest_score)
    totals = jnp.sum(exponent, axis=-1, keepdims=True)
    chances = (exponent / totals).astype(jnp.bfloat16)
    result = jnp.einsum("hij,jhd->ihd", chances, all_values, preferred_element_type=jnp.float32)
    return (result, highest_score + jnp.log(totals))


def attend_back(queries, all_keys, all_values, allowed, score_scale, logsum, grad_result):
    scores = scores_of(queries, all_keys, allowed, score_scale)
    chances = jnp.exp(scores - logsum)
    grad_chances = jnp.einsum(
        "ihd,jhd->hij", grad_result, all_values, preferred_element_type=jnp.float32
    )
    row_dot = jnp.sum(chances * grad_chances, axis=-1, keepdims=True)
    grad_scores = (chances * (grad_chances - row_dot)).astype(jnp.bfloat16)
    grad_values = jnp.einsum(
        "hij,ihd->jhd",
        chances.astype(jnp.bfloat16),
        grad_result,
        preferred_element_type=jnp.float32,
    )
    grad_queries = (
        jnp.einsum("hij,jhd->ihd", grad_scores, all_keys, preferred_element_type=jnp.float32)
        * score_scale
    )
    grad_keys = (
        jnp.einsum("hij,ihd->jhd", grad_scores, queries, preferred_element_type=jnp.float32)
        * score_scale
    )
    return (grad_queries, grad_keys, grad_values)


def gelu_tanh(inner):
    return jax.nn.gelu(inner, approximate=True)


def shards(
    tokens,
    branch,
    w_attn,
    w_proj,
    w_expand,
    w_contract,
    attn_bias,
    branch_bias,
    expand_bias,
    norm_gains,
    norm_shifts,
    cotangent,
):
    seq_count = lax.axis_size("seq")
    seq_index = lax.axis_index("seq")
    tensor_count = lax.axis_size("tensor")
    tensor_index = lax.axis_index("tensor")
    width = tokens.shape[3]
    row_count = tokens.shape[2]
    share = row_count // tensor_count
    row_start = tensor_index * share
    local_width = w_attn.shape[2]
    local_heads = local_width // HEAD_DIM
    prompt = PCH * seq_count
    score_scale = 1.0 / math.sqrt(HEAD_DIM)
    layer_scale = 1.0 / math.sqrt(LAYERS)

    def rows_of(whole):
        return lax.dynamic_slice_in_dim(whole, row_start, share, 0)

    flat_rows = tokens.reshape(row_count, width).astype(jnp.float32)
    grad_out = cotangent.reshape(row_count, width).astype(jnp.float32)
    normed_one = layer_norm(flat_rows, norm_gains[0], norm_shifts[0]).astype(jnp.bfloat16)
    projected = jnp.einsum("rd,cde->cre", normed_one, w_attn, preferred_element_type=jnp.float32)
    bias_rows = jnp.stack([attn_bias[0], jnp.zeros_like(attn_bias[0]), attn_bias[1]])
    projected = (projected + bias_rows[:, None, :]).astype(jnp.bfloat16)
    query_flat, key_flat, value_flat = (projected[0], projected[1], projected[2])
    gathered_keys, gathered_values = (
        lax.all_gather(key_flat[:PCH], "seq", axis=0, tiled=True),
        lax.all_gather(value_flat[:PCH], "seq", axis=0, tiled=True),
    )

    def heads_of(flat):
        return flat.reshape(flat.shape[0], local_heads, HEAD_DIM)

    query_prompt = heads_of(query_flat[:PCH])
    query_cont = heads_of(query_flat[PCH:])
    places = jnp.arange(prompt)
    positions = seq_index * PCH + jnp.arange(PCH)
    allowed_prompt = places[None, :] <= positions[:, None]
    cont_places = jnp.arange(CLEN)
    branch_end = branch[0, 0]
    allowed_cont = jnp.concatenate(
        [
            jnp.broadcast_to(places[None, :] < branch_end, (CLEN, prompt)),
            cont_places[None, :] <= cont_places[:, None],
        ],
        axis=1,
    )
    keys_prompt = heads_of(gathered_keys)
    values_prompt = heads_of(gathered_values)
    keys_cont = jnp.concatenate([keys_prompt, heads_of(key_flat[PCH:])], axis=0)
    values_cont = jnp.concatenate([values_prompt, heads_of(value_flat[PCH:])], axis=0)
    keys_prompt, values_prompt, keys_cont, values_cont = (
        keys_prompt,
        values_prompt,
        keys_cont,
        values_cont,
    )
    out_prompt, logsum_prompt = attend(
        query_prompt, keys_prompt, values_prompt, allowed_prompt, score_scale
    )
    out_cont, logsum_cont = attend(query_cont, keys_cont, values_cont, allowed_cont, score_scale)
    attended = (
        jnp.concatenate([out_prompt, out_cont], axis=0)
        .reshape(row_count, local_width)
        .astype(jnp.bfloat16)
    )
    attn_terms = jnp.dot(attended, w_proj, preferred_element_type=jnp.float32)
    attn_summed = lax.psum(attn_terms, "tensor")
    hidden = flat_rows + layer_scale * (attn_summed + branch_bias[0])
    normed_two = layer_norm(hidden, norm_gains[1], norm_shifts[1]).astype(jnp.bfloat16)
    preact = jnp.dot(normed_two, w_expand, preferred_element_type=jnp.float32) + expand_bias
    activated = gelu_tanh(preact).astype(jnp.bfloat16)
    contract_terms = jnp.dot(activated, w_contract, preferred_element_type=jnp.float32)
    mlp_summed = lax.psum(contract_terms.astype(jnp.bfloat16), "tensor").astype(jnp.float32)
    layer_out = rows_of((hidden + layer_scale * (mlp_summed + branch_bias[1])).astype(jnp.bfloat16))
    grad_mlp = (grad_out * layer_scale).astype(jnp.bfloat16)
    grad_contract = jnp.einsum("rf,rd->fd", activated, grad_mlp, preferred_element_type=jnp.float32)
    grad_activated = jnp.einsum(
        "rd,fd->rf", grad_mlp, w_contract, preferred_element_type=jnp.float32
    )
    gelu_value, gelu_back = jax.vjp(gelu_tanh, preact)
    grad_preact = gelu_back(grad_activated)[0].astype(jnp.bfloat16)
    grad_expand = jnp.einsum(
        "rd,rf->df", normed_two, grad_preact, preferred_element_type=jnp.float32
    )
    mixed_terms = jnp.einsum("rf,df->rd", grad_preact, w_expand, preferred_element_type=jnp.float32)
    grad_mixed = lax.psum(mixed_terms, "tensor")
    norm_value_two, norm_back_two = jax.vjp(layer_norm, hidden, norm_gains[1], norm_shifts[1])
    grad_hidden_norm, gain_two, shift_two = norm_back_two(grad_mixed)
    grad_hidden = grad_out + grad_hidden_norm
    grad_att = (grad_hidden * layer_scale).astype(jnp.bfloat16)
    grad_proj = jnp.einsum("re,rd->ed", attended, grad_att, preferred_element_type=jnp.float32)
    grad_attended = jnp.einsum(
        "rd,ed->re", grad_att, w_proj, preferred_element_type=jnp.float32
    ).astype(jnp.bfloat16)
    grad_attended = heads_of(grad_attended)
    grad_query_prompt, grad_key_pp, grad_value_pp = attend_back(
        query_prompt,
        keys_prompt,
        values_prompt,
        allowed_prompt,
        score_scale,
        logsum_prompt,
        grad_attended[:PCH],
    )
    grad_query_cont, grad_key_cont, grad_value_cont = attend_back(
        query_cont,
        keys_cont,
        values_cont,
        allowed_cont,
        score_scale,
        logsum_cont,
        grad_attended[PCH:],
    )
    prompt_key_terms = (grad_key_pp + grad_key_cont[:prompt]).reshape(prompt, local_width)
    prompt_value_terms = (grad_value_pp + grad_value_cont[:prompt]).reshape(prompt, local_width)
    own_keys, own_values = (
        lax.psum_scatter(prompt_key_terms, "seq", scatter_dimension=0, tiled=True),
        lax.psum_scatter(prompt_value_terms, "seq", scatter_dimension=0, tiled=True),
    )
    grad_keys = jnp.concatenate(
        [own_keys, grad_key_cont[prompt:].reshape(CLEN, local_width)], axis=0
    ).astype(jnp.bfloat16)
    grad_values = jnp.concatenate(
        [own_values, grad_value_cont[prompt:].reshape(CLEN, local_width)], axis=0
    ).astype(jnp.bfloat16)
    grad_queries = (
        jnp.concatenate([grad_query_prompt, grad_query_cont], axis=0)
        .reshape(row_count, local_width)
        .astype(jnp.bfloat16)
    )
    stacked = jnp.stack([grad_queries, grad_keys, grad_values])
    grad_attn = jnp.einsum("rd,cre->cde", normed_one, stacked, preferred_element_type=jnp.float32)
    normed_terms = jnp.einsum("cre,cde->rd", stacked, w_attn, preferred_element_type=jnp.float32)
    grad_normed = lax.psum(normed_terms, "tensor")
    norm_value_one, norm_back_one = jax.vjp(layer_norm, flat_rows, norm_gains[0], norm_shifts[0])
    grad_rows_norm, gain_one, shift_one = norm_back_one(grad_normed)
    grad_tokens = (grad_hidden + grad_rows_norm).astype(jnp.bfloat16)
    grad_tokens = rows_of(grad_tokens)
    bias_terms = jnp.stack(
        [
            jnp.sum(grad_queries.astype(jnp.float32), axis=0),
            jnp.sum(grad_values.astype(jnp.float32), axis=0),
        ]
    )
    branch_terms = jnp.stack(
        [
            jnp.sum(grad_att.astype(jnp.float32), axis=0),
            jnp.sum(grad_mlp.astype(jnp.float32), axis=0),
        ]
    )
    expand_terms = jnp.sum(grad_preact.astype(jnp.float32), axis=0)
    gain_terms = jnp.stack([gain_one, gain_two])
    shift_terms = jnp.stack([shift_one, shift_two])
    vectors = lax.psum(
        (bias_terms, branch_terms, expand_terms, gain_terms, shift_terms), ("dp", "seq")
    )
    reduced = (
        lax.psum_scatter(grad_attn, ("dp", "seq"), scatter_dimension=1, tiled=True),
        lax.psum_scatter(grad_proj, ("dp", "seq"), scatter_dimension=1, tiled=True),
        lax.psum_scatter(grad_expand, ("dp", "seq"), scatter_dimension=0, tiled=True),
        lax.psum_scatter(grad_contract, ("dp", "seq"), scatter_dimension=1, tiled=True),
    )
    out_shape = (1, 1, share, width)
    return (
        layer_out.reshape(out_shape),
        grad_tokens.reshape(out_shape),
        reduced[0],
        reduced[1],
        reduced[2],
        reduced[3],
        vectors[0],
        vectors[1],
        vectors[2],
        vectors[3],
        vectors[4],
    )


def solution(mesh):
    placed = (
        P("dp", "seq", None, None),
        P("dp", "seq"),
        P(None, None, "tensor"),
        P("tensor", None),
        P(None, "tensor"),
        P("tensor", None),
        P(None, "tensor"),
        P(),
        P("tensor"),
        P(),
        P(),
        P("dp", "seq", None, None),
    )
    return jax.shard_map(
        shards,
        mesh=mesh,
        in_specs=placed,
        out_specs=(
            P("dp", "seq", "tensor", None),
            P("dp", "seq", "tensor", None),
            P(None, ("dp", "seq"), "tensor"),
            P("tensor", ("dp", "seq")),
            P(("dp", "seq"), "tensor"),
            P("tensor", ("dp", "seq")),
            P(None, "tensor"),
            P(),
            P("tensor"),
            P(),
            P(),
        ),
        check_vma=False,
    )
```

profile of v0, /device:TPU:0, one launch (start us, length us, event | category | flops | bytes accessed | tf_op | source)
XLA Modules:
  0.0 758.0 jit_solution(15909318368735387643)
XLA Ops:
  16.5 21.3 %all-gather.1 = bf16[1,2048,192]{1,2,0:T(8,128)(2,1)S(1)} all-gather(bf16[1,512,192]{1,2,0:T(8,128)(2,1)S(1)} %get-tuple-element.65), channel_id=3, replica_groups=mesh['dp'=2,'seq'=4,'tensor'=4] {'seq'}, dimensions={1}, use_global_device_ids=true | all-gather | bytes 983040 | tf_op jit(solution)/shard_map/all_gather | solution.py:108
  37.8 17.9 %all-gather = bf16[1,2048,192]{1,2,0:T(8,128)(2,1)S(1)} all-gather(bf16[1,512,192]{1,2,0:T(8,128)(2,1)S(1)} %get-tuple-element.66), channel_id=2, replica_groups=mesh['dp'=2,'seq'=4,'tensor'=4] {'seq'}, dimensions={1}, use_global_device_ids=true | all-gather | bytes 983040 | tf_op jit(solution)/shard_map/all_gather | solution.py:109
  67.6 7.3 fusion.86
  74.9 7.7 %fusion = f32[3,512]{1,0:T(4,128)S(1)} fusion(f32[3,512,2560]{2,1,0:T(8,128)} %get-tuple-element.72, f32[3,512]{1,0:T(4,128)S(1)} %get-tuple-element.71), kind=kLoop, calls=%fused_computation.6 | loop fusion | flops 7862784 | bytes 15740928 | tf_op jit(solution)/shard_map/reduce_sum | solution.py:34
  82.7 7.1 fusion.61
  94.7 66.6 %all-reduce.6.cloned.1.call-done = f32[1024,768]{1,0:T(8,128)} async-done(((f32[1024,768]{1,0:T(8,128)}), f32[1024,768]{1,0:T(8,128)}) %all-reduce.6.cloned.1.call-update) | async-done | bytes 3145744 | tf_op jit(solution)/shard_map/psum | solution.py:149
  168.1 3.9 convert_reduce_fusion.1
  178.4 66.6 %all-reduce.10.cloned.1.call-done = f32[1024,768]{1,0:T(8,128)} async-done(((f32[1024,768]{1,0:T(8,128)}), f32[1024,768]{1,0:T(8,128)}) %all-reduce.10.cloned.1.call-update) | async-done | bytes 3145744 | tf_op jit(solution)/shard_map/psum | solution.py:168
  245.0 4.4 multiply_reduce_fusion.2
  255.0 9.8 %fusion.19 = f32[2560,3,64]{0,2,1:T(8,128)} fusion(bf16[512,3,64]{0,2,1:T(8,128)(2,1)S(1)} %bitcast.166, f32[3,512,2560]{2,1,0:T(8,128)} %get-tuple-element.72, f32[3,512]{1,0:T(4,128)S(1)} %log_add_fusion), kind=kOutput, calls=%fused_computation.40 | convolution fusion | flops 511180800 | bytes 17897472 | tf_op jit(solution)/shard_map/hij,ihd->jhd/dot_general | solution.py:48
  264.8 8.0 %multiply_reduce_fusion = (f32[3,512]{1,0:T(4,128)}, f32[3,512,2560]{2,1,0:T(8,128)}) fusion(f32[3,512,2560]{2,1,0:T(8,128)S(1)} %bitcast.148, f32[3,512]{1,0:T(4,128)S(1)} %log_add_fusion, bf16[512,3,64]{0,2,1:T(8,128)(2,1)S(1)} %bitcast.167, bf16[512,3,64]{0,2,1:T(8,128)(2,1)S(1)} %bitcast.173, bf16[2048,3,64]{0,2,1:T(8,128)(2,1)S(1)} %bitcast.154), kind=kOutput, calls=%fused_computation.1 | convolution fusion | flops 517077504 | bytes 32649216 | tf_op jit(solution)/shard_map/ihd,jhd->hij/dot_general | solution.py:43
  272.9 8.2 %fusion.42 = f32[2048,3,64]{0,2,1:T(8,128)} fusion(bf16[512,3,64]{0,2,1:T(8,128)(2,1)S(1)} %bitcast.169, f32[3,512,2048]{2,1,0:T(8,128)} %copy-done.1, f32[3,512]{1,0:T(4,128)S(1)} %log_add_fusion.1, f32[2560,3,64]{0,2,1:T(8,128)} %fusion.19), kind=kOutput, calls=%fused_computation.69 | convolution fusion | flops 409337856 | bytes 15931392 | tf_op jit(solution)/shard_map/hij,ihd->jhd/dot_general | solution.py:48
  281.4 11.6 %multiply_convert_fusion = bf16[3,512,2560]{2,1,0:T(8,128)(2,1)S(1)} fusion(f32[3,512,2560]{2,1,0:T(8,128)} %get-tuple-element.76, f32[3,512,2560]{2,1,0:T(8,128)} %get-tuple-element.72, f32[3,512]{1,0:T(4,128)} %get-tuple-element.75, f32[3,512]{1,0:T(4,128)S(1)} %log_add_fusion), kind=kLoop, calls=%fused_computation | loop fusion | flops 15728640 | bytes 39333888 | tf_op jit(solution)/shard_map/convert_element_type | solution.py:47
  298.8 6.5 multiply_reduce_fusion.1
  306.0 4.6 multiply_convert_fusion.1
  310.6 5.7 fusion.41
  316.4 5.2 convolution_convert_fusion
  325.3 6.5 fusion.50
  331.9 4.9 fusion.51
  340.7 12.6 %reduce-scatter.11.cloned.1.call-done = f32[512,192]{0,1:T(8,128)} async-done(((f32[2048,192]{0,1:T(8,128)}), f32[512,192]{0,1:T(8,128)}) %reduce-scatter.11.cloned.1.call-update) | async-done | bytes 393232 | tf_op jit(solution)/shard_map/reduce_scatter | solution.py:199
  355.0 4.4 convolution_bitcast_fusion
  363.7 4.3 copy.25
  368.0 4.7 reshape.300
  372.8 5.8 fusion.52
  378.7 4.8 fusion.91
  383.5 13.8 %all-reduce.8.cloned.1.call-done = bf16[1024,768]{1,0:T(8,128)(2,1)} async-done(((bf16[1024,768]{1,0:T(8,128)(2,1)}), bf16[1024,768]{1,0:T(8,128)(2,1)}) %all-reduce.8.cloned.1.call-update) | async-done | bytes 1572880 | tf_op jit(solution)/shard_map/psum | solution.py:155
  399.6 64.2 %reduce-scatter.21.cloned.1.call-done = f32[96,192]{1,0:T(8,128)} async-done(((f32[768,192]{1,0:T(8,128)}), f32[96,192]{1,0:T(8,128)}) %reduce-scatter.21.cloned.1.call-update) | async-done | bytes 73744
  465.6 68.1 %all-reduce.12.cloned.1.call-done = f32[1024,768]{1,0:T(8,128)} async-done(((f32[1024,768]{1,0:T(8,128)}), f32[1024,768]{1,0:T(8,128)}) %all-reduce.12.cloned.1.call-update) | async-done | bytes 3145744 | tf_op jit(solution)/shard_map/psum | solution.py:216
  539.5 38.3 %all-reduce = (f32[2,192]{1,0:T(2,128)}, f32[2,768]{1,0:T(2,128)}, f32[768]{0:T(1024)}, f32[2,768]{1,0:T(2,128)}, f32[2,768]{1,0:T(2,128)}) all-reduce(f32[2,192]{1,0:T(2,128)S(1)} %pad_maximum_fusion.11, f32[2,768]{1,0:T(2,128)S(1)} %pad_maximum_fusion.7, ...), channel_id=1, replica_groups=mesh['dp'=2,'seq'=4,'tensor'=4] {'dp','seq'}, use_global_device_ids=true, to_apply=%region_26.27 | all-reduce | flops 5760 | bytes 46080 | tf_op jit(solution)/shard_map/psum | solution.py:236
  580.0 25.5 %reduce-scatter.19.cloned.1.call-done = f32[96,576]{1,0:T(8,128)} async-done(((f32[768,576]{1,0:T(8,128)}), f32[96,576]{1,0:T(8,128)}) %reduce-scatter.19.cloned.1.call-update) | async-done | bytes 221200
  607.4 70.9 %reduce-scatter.17.cloned.1.call-done = f32[768,96]{0,1:T(8,128)} async-done(((f32[768,768]{0,1:T(8,128)}), f32[768,96]{0,1:T(8,128)}) %reduce-scatter.17.cloned.1.call-update) | async-done | bytes 294928 | tf_op jit(solution)/shard_map/reduce_scatter | solution.py:243
  678.3 72.7 %reduce-scatter.15.cloned.1.call-done = f32[96,768]{1,0:T(8,128)} async-done(((f32[768,768]{1,0:T(8,128)}), f32[96,768]{1,0:T(8,128)}) %reduce-scatter.15.cloned.1.call-update) | async-done | bytes 294928 | tf_op jit(solution)/shard_map/reduce_scatter | solution.py:242
  (242 shorter events, 78.3 us)
Async XLA Ops:
  7.2 160.9 %copy-start = (bf16[768,768]{1,0:T(8,128)(2,1)S(1)}, bf16[768,768]{1,0:T(8,128)(2,1)}, u32[]{:S(2)}) copy-start(bf16[768,768]{1,0:T(8,128)(2,1)} %param.17) | copy-start | bytes 3538948
  7.2 154.1 %all-reduce.6.cloned.1.call-start = ((), (), s32[]{:S(2)}) async-start(), calls=%async_computation.6 | async-start | bytes 6291456 | tf_op jit(solution)/shard_map/psum | solution.py:149
  14.1 150.2 %copy-start.35 = (f32[768]{0:T(1024)}, f32[768]{0:T(1024)S(1)}, u32[]{:S(2)}) copy-start(f32[768]{0:T(1024)S(1)} %get-tuple-element.82) | copy-start | bytes 9220
  15.6 40.1 %copy-start.23 = (pred[512,512]{1,0:T(8,128)(4,1)S(1)}, pred[512,512]{1,0:T(8,128)(4,1)}, u32[]{:S(2)}) copy-start(pred[512,512]{1,0:T(8,128)(4,1)} %iota_compare_fusion.1) | copy-start | bytes 786436
  16.5 43.3 %copy-start.27 = (bf16[1,512,192]{1,2,0:T(8,128)(2,1)}, bf16[1,512,192]{1,2,0:T(8,128)(2,1)S(1)}, u32[]{:S(2)}) copy-start(bf16[1,512,192]{1,2,0:T(8,128)(2,1)S(1)} %get-tuple-element.61) | copy-start | bytes 589828
  16.5 51.1 %copy-start.12 = (bf16[1,512,192]{1,2,0:T(8,128)(2,1)}, bf16[1,512,192]{1,2,0:T(8,128)(2,1)S(1)}, u32[]{:S(2)}) copy-start(bf16[1,512,192]{1,2,0:T(8,128)(2,1)S(1)} %get-tuple-element.63) | copy-start | bytes 589828
  16.5 66.1 %copy-start.24 = (bf16[1,512,192]{1,2,0:T(8,128)(2,1)}, bf16[1,512,192]{1,2,0:T(8,128)(2,1)S(1)}, u32[]{:S(2)}) copy-start(bf16[1,512,192]{1,2,0:T(8,128)(2,1)S(1)} %get-tuple-element.64) | copy-start | bytes 589828
  37.8 29.8 %copy-start.9 = (bf16[1,2048,192]{1,2,0:T(8,128)(2,1)}, bf16[1,2048,192]{1,2,0:T(8,128)(2,1)S(1)}, u32[]{:S(2)}) copy-start(bf16[1,2048,192]{1,2,0:T(8,128)(2,1)S(1)} %all-gather.1) | copy-start | bytes 2359300
  92.9 152.1 %all-reduce.10.cloned.1.call-start = ((), (), s32[]{:S(2)}) async-start(), calls=%async_computation.8 | async-start | bytes 6291456 | tf_op jit(solution)/shard_map/psum | solution.py:168
  176.3 162.7 %reduce-scatter.13.cloned.1.call-start = ((), (), s32[]{:S(2)}) async-start(), calls=%async_computation.10 | async-start | bytes 1966080 | tf_op jit(solution)/shard_map/reduce_scatter | solution.py:200
  254.2 10.6 %slice-start = ((s8[15728640]{0:T(1024)(128)(4,1)}), s8[4194304]{0:T(1024)(128)(4,1)S(1)}, s32[]{:S(2)}) async-start(s8[15728640]{0:T(1024)(128)(4,1)} %bitcast.147), calls=%async_computation.16 | async-start | bytes 8388608
  254.9 18.0 %copy-start.14 = (bf16[512,192]{0,1:T(8,128)(2,1)}, bf16[512,192]{0,1:T(8,128)(2,1)S(1)}, u32[]{:S(2)}) copy-start(bf16[512,192]{0,1:T(8,128)(2,1)S(1)} %get-tuple-element.67) | copy-start | bytes 589828
  254.9 9.9 %slice-start.1 = ((s8[15728640]{0:T(1024)(128)(4,1)}), s8[4194304]{0:T(1024)(128)(4,1)S(1)}, s32[]{:S(2)}) async-start(s8[15728640]{0:T(1024)(128)(4,1)} %bitcast.147), calls=%async_computation.17 | async-start | bytes 8388608
  254.9 9.9 %slice-start.2 = ((s8[15728640]{0:T(1024)(128)(4,1)}), s8[4194304]{0:T(1024)(128)(4,1)S(1)}, s32[]{:S(2)}) async-start(s8[15728640]{0:T(1024)(128)(4,1)} %bitcast.147), calls=%async_computation.18 | async-start | bytes 8388608
  254.9 9.9 %slice-start.3 = ((s8[15728640]{0:T(1024)(128)(4,1)}), s8[3145728]{0:T(1024)(128)(4,1)S(1)}, s32[]{:S(2)}) async-start(s8[15728640]{0:T(1024)(128)(4,1)} %bitcast.147), calls=%async_computation.19 | async-start | bytes 6291456
  255.0 9.9 %copy-start.25 = (bf16[1,512,192]{1,2,0:T(8,128)(2,1)S(1)}, bf16[1,512,192]{1,2,0:T(8,128)(2,1)}, u32[]{:S(2)}) copy-start(bf16[1,512,192]{1,2,0:T(8,128)(2,1)} %copy-done.24) | copy-start | bytes 589828
  281.2 72.2 %reduce-scatter.11.cloned.1.call-start = ((), (), s32[]{:S(2)}) async-start(), calls=%async_computation.9 | async-start | bytes 1966080 | tf_op jit(solution)/shard_map/reduce_scatter | solution.py:199
  281.4 14.6 %copy-start.13 = (bf16[1,512,192]{1,2,0:T(8,128)(2,1)S(1)}, bf16[1,512,192]{1,2,0:T(8,128)(2,1)}, u32[]{:S(2)}) copy-start(bf16[1,512,192]{1,2,0:T(8,128)(2,1)} %copy-done.12) | copy-start | bytes 589828
  296.0 9.3 %slice-start.4 = ((s8[12582912]{0:T(1024)(128)(4,1)}), s8[4194304]{0:T(1024)(128)(4,1)S(1)}, s32[]{:S(2)}) async-start(s8[12582912]{0:T(1024)(128)(4,1)} %bitcast.149), calls=%async_computation.20 | async-start | bytes 8388608
  316.3 81.0 %all-reduce.8.cloned.1.call-start = ((), (), s32[]{:S(2)}) async-start(), calls=%async_computation.7 | async-start | bytes 3145728 | tf_op jit(solution)/shard_map/psum | solution.py:155
  321.6 142.2 %reduce-scatter.21.cloned.1.call-start = ((), (), s32[]{:S(2)}) async-start(), calls=%async_computation.15 | async-start | bytes 884736
  331.8 201.8 %all-reduce.12.cloned.1.call-start = ((), (), s32[]{:S(2)}) async-start(), calls=%async_computation.11 | async-start | bytes 6291456 | tf_op jit(solution)/shard_map/psum | solution.py:216
  359.5 246.0 %reduce-scatter.19.cloned.1.call-start = ((), (), s32[]{:S(2)}) async-start(), calls=%async_computation.14 | async-start | bytes 2211840
  372.7 305.6 %reduce-scatter.17.cloned.1.call-start = ((), (), s32[]{:S(2)}) async-start(), calls=%async_computation.13 | async-start | bytes 2654208 | tf_op jit(solution)/shard_map/reduce_scatter | solution.py:243
  378.6 18.7 %copy-start.52 = (f32[768]{0:T(1024)S(1)}, f32[768]{0:T(1024)}, u32[]{:S(2)}) copy-start(f32[768]{0:T(1024)} %get-tuple-element.43) | copy-start | bytes 9220
  378.6 372.3 %reduce-scatter.15.cloned.1.call-start = ((), (), s32[]{:S(2)}) async-start(), calls=%async_computation.12 | async-start | bytes 2654208 | tf_op jit(solution)/shard_map/reduce_scatter | solution.py:242
  383.5 15.9 %copy-start.54 = (f32[768]{0:T(1024)S(1)}, f32[768]{0:T(1024)}, u32[]{:S(2)}) copy-start(f32[768]{0:T(1024)} %get-tuple-element.33) | copy-start | bytes 9220
  383.5 15.9 %copy-start.53 = (f32[768]{0:T(1024)S(1)}, f32[768]{0:T(1024)}, u32[]{:S(2)}) copy-start(f32[768]{0:T(1024)} %get-tuple-element.38) | copy-start | bytes 9220
  383.5 15.9 %copy-start.56 = (f32[768]{0:T(1024)S(1)}, f32[768]{0:T(1024)}, u32[]{:S(2)}) copy-start(f32[768]{0:T(1024)} %get-tuple-element.50) | copy-start | bytes 9220
  383.5 16.0 %copy-start.55 = (f32[768]{0:T(1024)S(1)}, f32[768]{0:T(1024)}, u32[]{:S(2)}) copy-start(f32[768]{0:T(1024)} %get-tuple-element.60) | copy-start | bytes 9220
  383.5 81.9 %copy-start.16 = (f32[512,192]{0,1:T(8,128)S(1)}, f32[512,192]{0,1:T(8,128)}, u32[]{:S(2)}) copy-start(f32[512,192]{0,1:T(8,128)} %reduce-scatter.13.cloned.1.call-done) | copy-start | bytes 1179652
  399.4 137.3 %copy-start.44 = (f32[1024]{0:T(1024)S(1)}, f32[1024]{0:T(1024)}, u32[]{:S(2)}) copy-start(f32[1024]{0:T(1024)} %copy-done.43) | copy-start | bytes 12292
  (53 other events, 186.8 us)
Sparse Core Ops, SparseCore 0:
  93.0 68.2 all-reduce.5
  176.4 68.5 all-reduce.9
  281.3 35.5 reduce-scatter.12
  319.0 34.2 reduce-scatter.10
  355.5 41.6 all-reduce.7
  400.4 63.2 reduce-scatter.20
  466.1 67.4 all-reduce.11
  537.1 68.3 reduce-scatter.18
  609.6 68.6 reduce-scatter.16
  682.2 68.7 reduce-scatter.14
where the time goes:
time: 762 us; the launch traced here: 758 us
  waiting for transfers between devices  461 us (60%)
  matrix products  113 us (15%)
  blocking collectives  77.5 us (10%)
  other arithmetic  57.9 us (8%)
  local copies, waits for them, and re-layouts  31.7 us (4%)
  between operations  16 us (2%)
    unnamed x12, waiting for transfers between devices  89.8 us
    reduce_scatter x1, waiting for transfers between devices, shards(): lax.psum_scatter(grad_expand, ('dp', 'seq'), scatter_dimension=0, tiled=T...  72.7 us
    reduce_scatter x1, waiting for transfers between devices, shards(): lax.psum_scatter(grad_contract, ('dp', 'seq'), scatter_dimension=1, tiled...  70.9 us
    psum x1, waiting for transfers between devices, shards(): grad_normed = lax.psum(normed_terms, 'tensor')  68.1 us
    psum x1, waiting for transfers between devices, shards(): attn_summed = lax.psum(attn_terms, 'tensor')  66.6 us
    psum x1, waiting for transfers between devices, shards(): grad_mixed = lax.psum(mixed_terms, 'tensor')  66.6 us
    psum x1, blocking collectives, shards(): lax.psum((bias_terms, branch_terms, expand_terms, gain_terms, shift_terms...  38.3 us
    unnamed x155, local copies, waits for them, and re-layouts  26.4 us
  transfers between devices with their start and end apart: 10, of which 9 were waited for; matrix products, arithmetic and copies ran while one was open for 13% of the time, Pallas kernels for 0%

commit v1 on v0

--- a/solution.py
+++ b/solution.py
@@ -1,3 +1,4 @@
+import functools
 import math
 import jax
 import jax.numpy as jnp
@@ -10,6 +11,41 @@
 CLEN = 512
 norm_eps = 1e-05
 big_negative = -1000000000.0
+
+
+def reach_records_here(piece_in, link_axis):
+    n_now, carry_in, x_new = (
+        lax.axis_size(link_axis),
+        lax.axis_index(link_axis),
+        piece_in.shape[0],
+    )
+    found = []
+    for no, tick in enumerate(piece_in.shape):
+        found.append(tick * n_now if no == 0 else tick)
+    spare = lax.dynamic_update_slice_in_dim(
+        jnp.zeros(found, piece_in.dtype), piece_in, carry_in * x_new, axis=0
+    )
+    small = everything = piece_in
+    for w in range(1, n_now // 2 + 1):
+        sides = []
+        for no in range(n_now):
+            sides.append((no, (no + 1) % n_now))
+        small = lax.ppermute(small, link_axis, sides)
+        spare = lax.dynamic_update_slice_in_dim(
+            spare, small, (carry_in - w) % n_now * x_new, axis=0
+        )
+        if 2 * w < n_now:
+            pile = []
+            for no in range(n_now):
+                pile.append((no, (no - 1) % n_now))
+            everything = lax.ppermute(everything, link_axis, pile)
+            spare = lax.dynamic_update_slice_in_dim(
+                spare, everything, (carry_in + w) % n_now * x_new, axis=0
+            )
+    return spare
+
+
+close_cycles = functools.partial(reach_records_here, link_axis="seq")
 
 
 def layer_norm(value, gain, shift):
@@ -106,7 +142,7 @@
     query_flat, key_flat, value_flat = (projected[0], projected[1], projected[2])
     gathered_keys, gathered_values = (
         lax.all_gather(key_flat[:PCH], "seq", axis=0, tiled=True),
-        lax.all_gather(value_flat[:PCH], "seq", axis=0, tiled=True),
+        close_cycles(value_flat[:PCH]),
     )
 
     def heads_of(flat):

time: 762 us -> 762 us (level)
  blocking collectives: 77.5 us -> 57.4 us
    all_gather x1 -> x0, blocking collectives: 17.9 us -> none  [shards(): lax.all_gather(value_flat[:PCH], 'seq', axis=0, tiled=True)]
    unnamed x155 -> x157, local copies, waits for them, and re-layouts: 26.4 us -> 27.6 us
  transfers between devices with their start and end apart: 10 -> 13, of which waited for: 9 -> 10; matrix products, arithmetic and copies ran while one was open for 13% -> 17% of each run, Pallas kernels for 0% -> 0%
where the time goes in v1:
time: 762 us; the launch traced here: 757 us
  waiting for transfers between devices  465 us (61%)
  matrix products  115 us (15%)
  other arithmetic  60.9 us (8%)
  blocking collectives  57.4 us (8%)
  local copies, waits for them, and re-layouts  36.3 us (5%)
  between operations  16 us (2%)
    unnamed x12, waiting for transfers between devices  89.9 us
    reduce_scatter x1, waiting for transfers between devices, shards(): lax.psum_scatter(grad_expand, ('dp', 'seq'), scatter_dimension=0, tiled=T...  72.8 us
    reduce_scatter x1, waiting for transfers between devices, shards(): lax.psum_scatter(grad_contract, ('dp', 'seq'), scatter_dimension=1, tiled...  70.7 us
    psum x1, waiting for transfers between devices, shards(): grad_normed = lax.psum(normed_terms, 'tensor')  68.1 us
    psum x1, waiting for transfers between devices, shards(): grad_mixed = lax.psum(mixed_terms, 'tensor')  66.6 us
    psum x1, waiting for transfers between devices, shards(): attn_summed = lax.psum(attn_terms, 'tensor')  65.4 us
    psum x1, blocking collectives, shards(): lax.psum((bias_terms, branch_terms, expand_terms, gain_terms, shift_terms...  38.3 us
    unnamed x157, local copies, waits for them, and re-layouts  27.6 us
  transfers between devices with their start and end apart: 13, of which 10 were waited for; matrix products, arithmetic and copies ran while one was open for 17% of the time, Pallas kernels for 0%

profile of v1, /device:TPU:0, one launch (start us, length us, event | category | flops | bytes accessed | tf_op | source)
XLA Modules:
  0.0 757.4 jit_solution(14261759236367637118)
XLA Ops:
  24.5 19.1 %all-gather = bf16[1,2048,192]{1,2,0:T(8,128)(2,1)S(1)} all-gather(bf16[1,512,192]{1,2,0:T(8,128)(2,1)} %get-tuple-element.65), channel_id=2, replica_groups=mesh['dp'=2,'seq'=4,'tensor'=4] {'seq'}, dimensions={1}, use_global_device_ids=true | all-gather | bytes 983040 | tf_op jit(solution)/shard_map/all_gather | solution.py:144
  45.2 4.0 fusion.87
  53.7 8.2 %fusion.86 = (f32[3,512]{1,0:T(4,128)S(1)}, f32[3,512,2560]{2,1,0:T(8,128)}) fusion(bf16[512,3,64]{0,2,1:T(8,128)(2,1)S(1)} %bitcast.170, bf16[512,3,64]{0,2,1:T(8,128)(2,1)} %bitcast.183, bf16[2048,3,64]{0,2,1:T(8,128)(2,1)S(1)} %bitcast.163, pred[512,2560]{1,0:T(8,128)(4,1)S(1)} %pad_add_fusion), kind=kOutput, calls=%fused_computation.151 | convolution fusion | flops 517077504 | bytes 18225152 | tf_op jit(solution)/shard_map/ihd,jhd->hij/dot_general | solution.py:60
  61.9 8.3 %fusion = f32[3,512]{1,0:T(4,128)} fusion(f32[3,512,2560]{2,1,0:T(8,128)} %get-tuple-element.72, f32[3,512]{1,0:T(4,128)S(1)} %get-tuple-element.71), kind=kLoop, calls=%fused_computation.6 | loop fusion | flops 7862784 | bytes 15740928 | tf_op jit(solution)/shard_map/reduce_sum | solution.py:70
  73.6 5.6 collective-permute-done.2
  79.3 7.1 fusion.62
  95.3 65.4 %all-reduce.6.cloned.1.call-done = f32[1024,768]{1,0:T(8,128)} async-done(((f32[1024,768]{1,0:T(8,128)}), f32[1024,768]{1,0:T(8,128)}) %all-reduce.6.cloned.1.call-update) | async-done | bytes 3145744 | tf_op jit(solution)/shard_map/psum | solution.py:185
  177.7 66.6 %all-reduce.10.cloned.1.call-done = f32[1024,768]{1,0:T(8,128)} async-done(((f32[1024,768]{1,0:T(8,128)}), f32[1024,768]{1,0:T(8,128)}) %all-reduce.10.cloned.1.call-update) | async-done | bytes 3145744 | tf_op jit(solution)/shard_map/psum | solution.py:204
  244.4 4.4 multiply_reduce_fusion.2
  254.4 9.8 %fusion.19 = f32[2560,3,64]{0,2,1:T(8,128)} fusion(bf16[512,3,64]{0,2,1:T(8,128)(2,1)S(1)} %bitcast.172, f32[3,512,2560]{2,1,0:T(8,128)} %get-tuple-element.72, f32[3,512]{1,0:T(4,128)S(1)} %log_add_fusion), kind=kOutput, calls=%fused_computation.40 | convolution fusion | flops 511180800 | bytes 17897472 | tf_op jit(solution)/shard_map/hij,ihd->jhd/dot_general | solution.py:84
  264.3 8.1 %multiply_reduce_fusion = (f32[3,512]{1,0:T(4,128)}, f32[3,512,2560]{2,1,0:T(8,128)}) fusion(f32[3,512,2560]{2,1,0:T(8,128)S(1)} %bitcast.154, f32[3,512]{1,0:T(4,128)S(1)} %log_add_fusion, bf16[512,3,64]{0,2,1:T(8,128)(2,1)S(1)} %bitcast.173, bf16[512,3,64]{0,2,1:T(8,128)(2,1)S(1)} %bitcast.179, bf16[2048,3,64]{0,2,1:T(8,128)(2,1)S(1)} %bitcast.160), kind=kOutput, calls=%fused_computation.1 | convolution fusion | flops 517077504 | bytes 32649216 | tf_op jit(solution)/shard_map/ihd,jhd->hij/dot_general | solution.py:79
  272.3 8.3 %fusion.42 = f32[2048,3,64]{0,2,1:T(8,128)} fusion(bf16[512,3,64]{0,2,1:T(8,128)(2,1)S(1)} %bitcast.175, f32[3,512,2048]{2,1,0:T(8,128)} %copy-done.1, f32[3,512]{1,0:T(4,128)S(1)} %log_add_fusion.1, f32[2560,3,64]{0,2,1:T(8,128)} %fusion.19), kind=kOutput, calls=%fused_computation.69 | convolution fusion | flops 409337856 | bytes 15931392 | tf_op jit(solution)/shard_map/hij,ihd->jhd/dot_general | solution.py:84
  281.1 11.6 %multiply_convert_fusion = bf16[3,512,2560]{2,1,0:T(8,128)(2,1)S(1)} fusion(f32[3,512,2560]{2,1,0:T(8,128)} %get-tuple-element.76, f32[3,512,2560]{2,1,0:T(8,128)} %get-tuple-element.72, f32[3,512]{1,0:T(4,128)} %get-tuple-element.75, f32[3,512]{1,0:T(4,128)S(1)} %log_add_fusion), kind=kLoop, calls=%fused_computation | loop fusion | flops 15728640 | bytes 39333888 | tf_op jit(solution)/shard_map/convert_element_type | solution.py:83
  298.5 6.5 multiply_reduce_fusion.1
  305.7 4.7 multiply_convert_fusion.1
  310.3 5.7 fusion.41
  316.1 5.2 convolution_convert_fusion
  325.1 6.5 fusion.50
  331.7 4.9 fusion.51
  340.5 12.3 %reduce-scatter.11.cloned.1.call-done = f32[512,192]{0,1:T(8,128)} async-done(((f32[2048,192]{0,1:T(8,128)}), f32[512,192]{0,1:T(8,128)}) %reduce-scatter.11.cloned.1.call-update) | async-done | bytes 393232 | tf_op jit(solution)/shard_map/reduce_scatter | solution.py:235
  354.5 4.4 convolution_bitcast_fusion
  363.1 4.3 copy.25
  367.4 4.7 reshape.298
  372.2 5.8 fusion.52
  378.1 4.8 fusion.91
  383.0 13.8 %all-reduce.8.cloned.1.call-done = bf16[1024,768]{1,0:T(8,128)(2,1)} async-done(((bf16[1024,768]{1,0:T(8,128)(2,1)}), bf16[1024,768]{1,0:T(8,128)(2,1)}) %all-reduce.8.cloned.1.call-update) | async-done | bytes 1572880 | tf_op jit(solution)/shard_map/psum | solution.py:191
  399.0 64.2 %reduce-scatter.21.cloned.1.call-done = f32[96,192]{1,0:T(8,128)} async-done(((f32[768,192]{1,0:T(8,128)}), f32[96,192]{1,0:T(8,128)}) %reduce-scatter.21.cloned.1.call-update) | async-done | bytes 73744
  465.1 68.1 %all-reduce.12.cloned.1.call-done = f32[1024,768]{1,0:T(8,128)} async-done(((f32[1024,768]{1,0:T(8,128)}), f32[1024,768]{1,0:T(8,128)}) %all-reduce.12.cloned.1.call-update) | async-done | bytes 3145744 | tf_op jit(solution)/shard_map/psum | solution.py:252
  538.9 38.3 %all-reduce = (f32[2,192]{1,0:T(2,128)}, f32[2,768]{1,0:T(2,128)}, f32[768]{0:T(1024)}, f32[2,768]{1,0:T(2,128)}, f32[2,768]{1,0:T(2,128)}) all-reduce(f32[2,192]{1,0:T(2,128)S(1)} %pad_maximum_fusion.11, f32[2,768]{1,0:T(2,128)S(1)} %pad_maximum_fusion.7, ...), channel_id=1, replica_groups=mesh['dp'=2,'seq'=4,'tensor'=4] {'dp','seq'}, use_global_device_ids=true, to_apply=%region_26.27 | all-reduce | flops 5760 | bytes 46080 | tf_op jit(solution)/shard_map/psum | solution.py:272
  579.5 25.5 %reduce-scatter.19.cloned.1.call-done = f32[96,576]{1,0:T(8,128)} async-done(((f32[768,576]{1,0:T(8,128)}), f32[96,576]{1,0:T(8,128)}) %reduce-scatter.19.cloned.1.call-update) | async-done | bytes 221200
  606.9 70.7 %reduce-scatter.17.cloned.1.call-done = f32[768,96]{0,1:T(8,128)} async-done(((f32[768,768]{0,1:T(8,128)}), f32[768,96]{0,1:T(8,128)}) %reduce-scatter.17.cloned.1.call-update) | async-done | bytes 294928 | tf_op jit(solution)/shard_map/reduce_scatter | solution.py:279
  677.6 72.8 %reduce-scatter.15.cloned.1.call-done = f32[96,768]{1,0:T(8,128)} async-done(((f32[768,768]{1,0:T(8,128)}), f32[96,768]{1,0:T(8,128)}) %reduce-scatter.15.cloned.1.call-update) | async-done | bytes 294928 | tf_op jit(solution)/shard_map/reduce_scatter | solution.py:278
  (255 shorter events, 92.0 us)
Async XLA Ops:
  7.2 160.3 %copy-start = (bf16[768,768]{1,0:T(8,128)(2,1)S(1)}, bf16[768,768]{1,0:T(8,128)(2,1)}, u32[]{:S(2)}) copy-start(bf16[768,768]{1,0:T(8,128)(2,1)} %param.17) | copy-start | bytes 3538948
  7.2 153.4 %all-reduce.6.cloned.1.call-start = ((), (), s32[]{:S(2)}) async-start(), calls=%async_computation.6 | async-start | bytes 6291456 | tf_op jit(solution)/shard_map/psum | solution.py:185
  12.6 151.0 %copy-start.32 = (f32[768]{0:T(1024)}, f32[768]{0:T(1024)S(1)}, u32[]{:S(2)}) copy-start(f32[768]{0:T(1024)S(1)} %get-tuple-element.82) | copy-start | bytes 9220
  16.3 55.0 %collective-permute-start = (bf16[512,192]{0,1:T(8,128)(2,1)}, bf16[512,192]{0,1:T(8,128)(2,1)}, u32[]{:S(2)}, u32[]{:S(2)}) collective-permute-start(bf16[512,192]{0,1:T(8,128)(2,1)} %get-tuple-element.66), channel_id=1, source_target_pairs={{0,4},{4,8},{8,12},{12,0},{1,5},{5,9},{9,13},{13,1},{2,6},{6,10},{... | collective-permute-start | bytes 589832 | tf_op jit(solution)/shard_map/ppermute | solution.py:33
  19.3 53.2 %collective-permute-start.1 = (bf16[512,192]{0,1:T(8,128)(2,1)}, bf16[512,192]{0,1:T(8,128)(2,1)}, u32[]{:S(2)}, u32[]{:S(2)}) collective-permute-start(bf16[512,192]{0,1:T(8,128)(2,1)} %get-tuple-element.66), channel_id=1, source_target_pairs={{0,12},{4,0},{8,4},{12,8},{1,13},{5,1},{9,5},{13,9},{2,14},{6,2},{... | collective-permute-start | bytes 589832 | tf_op jit(solution)/shard_map/ppermute | solution.py:41
  43.6 10.2 %copy-start.9 = (bf16[1,2048,192]{1,2,0:T(8,128)(2,1)}, bf16[1,2048,192]{1,2,0:T(8,128)(2,1)S(1)}, u32[]{:S(2)}) copy-start(bf16[1,2048,192]{1,2,0:T(8,128)(2,1)S(1)} %all-gather) | copy-start | bytes 2359300
  49.1 30.1 %copy-start.44 = (f32[3,512]{1,0:T(4,128)}, f32[3,512]{1,0:T(4,128)S(1)}, u32[]{:S(2)}) copy-start(f32[3,512]{1,0:T(4,128)S(1)} %get-tuple-element.73) | copy-start | bytes 18436
  71.3 7.9 %collective-permute-start.2 = (bf16[512,192]{0,1:T(8,128)(2,1)}, bf16[512,192]{0,1:T(8,128)(2,1)S(1)}, u32[]{:S(2)}, u32[]{:S(2)}) collective-permute-start(bf16[512,192]{0,1:T(8,128)(2,1)} %collective-permute-done), channel_id=1, source_target_pairs={{0,4},{4,8},{8,12},{12,0},{1,5},{5,9},{9,13},{13,1},{2,6},{6,10},{... | collective-permute-start | bytes 589832 | tf_op jit(solution)/shard_map/ppermute | solution.py:33
  72.5 13.9 %slice-start = ((s8[15728640]{0:T(1024)(128)(4,1)}), s8[4194304]{0:T(1024)(128)(4,1)S(1)}, s32[]{:S(2)}) async-start(s8[15728640]{0:T(1024)(128)(4,1)} %bitcast.151), calls=%async_computation.16 | async-start | bytes 8388608
  93.9 150.5 %all-reduce.10.cloned.1.call-start = ((), (), s32[]{:S(2)}) async-start(), calls=%async_computation.8 | async-start | bytes 6291456 | tf_op jit(solution)/shard_map/psum | solution.py:204
  175.6 163.2 %reduce-scatter.13.cloned.1.call-start = ((), (), s32[]{:S(2)}) async-start(), calls=%async_computation.10 | async-start | bytes 1966080 | tf_op jit(solution)/shard_map/reduce_scatter | solution.py:236
  253.6 10.6 %slice-start.4 = ((s8[15728640]{0:T(1024)(128)(4,1)}), s8[4194304]{0:T(1024)(128)(4,1)S(1)}, s32[]{:S(2)}) async-start(s8[15728640]{0:T(1024)(128)(4,1)} %bitcast.153), calls=%async_computation.20 | async-start | bytes 8388608
  254.3 18.0 %copy-start.15 = (bf16[512,192]{0,1:T(8,128)(2,1)}, bf16[512,192]{0,1:T(8,128)(2,1)S(1)}, u32[]{:S(2)}) copy-start(bf16[512,192]{0,1:T(8,128)(2,1)S(1)} %get-tuple-element.67) | copy-start | bytes 589828
  254.4 9.9 %slice-start.5 = ((s8[15728640]{0:T(1024)(128)(4,1)}), s8[4194304]{0:T(1024)(128)(4,1)S(1)}, s32[]{:S(2)}) async-start(s8[15728640]{0:T(1024)(128)(4,1)} %bitcast.153), calls=%async_computation.21 | async-start | bytes 8388608
  254.4 9.9 %slice-start.6 = ((s8[15728640]{0:T(1024)(128)(4,1)}), s8[4194304]{0:T(1024)(128)(4,1)S(1)}, s32[]{:S(2)}) async-start(s8[15728640]{0:T(1024)(128)(4,1)} %bitcast.153), calls=%async_computation.22 | async-start | bytes 8388608
  254.4 9.9 %slice-start.7 = ((s8[15728640]{0:T(1024)(128)(4,1)}), s8[3145728]{0:T(1024)(128)(4,1)S(1)}, s32[]{:S(2)}) async-start(s8[15728640]{0:T(1024)(128)(4,1)} %bitcast.153), calls=%async_computation.23 | async-start | bytes 6291456
  254.4 9.9 %copy-start.24 = (bf16[1,512,192]{1,2,0:T(8,128)(2,1)S(1)}, bf16[1,512,192]{1,2,0:T(8,128)(2,1)}, u32[]{:S(2)}) copy-start(bf16[1,512,192]{1,2,0:T(8,128)(2,1)} %get-tuple-element.64) | copy-start | bytes 589828
  280.6 72.2 %reduce-scatter.11.cloned.1.call-start = ((), (), s32[]{:S(2)}) async-start(), calls=%async_computation.9 | async-start | bytes 1966080 | tf_op jit(solution)/shard_map/reduce_scatter | solution.py:235
  281.1 14.6 %copy-start.14 = (bf16[1,512,192]{1,2,0:T(8,128)(2,1)S(1)}, bf16[1,512,192]{1,2,0:T(8,128)(2,1)}, u32[]{:S(2)}) copy-start(bf16[1,512,192]{1,2,0:T(8,128)(2,1)} %get-tuple-element.63) | copy-start | bytes 589828
  316.0 80.7 %all-reduce.8.cloned.1.call-start = ((), (), s32[]{:S(2)}) async-start(), calls=%async_computation.7 | async-start | bytes 3145728 | tf_op jit(solution)/shard_map/psum | solution.py:191
  321.3 141.9 %reduce-scatter.21.cloned.1.call-start = ((), (), s32[]{:S(2)}) async-start(), calls=%async_computation.15 | async-start | bytes 884736
  331.7 201.5 %all-reduce.12.cloned.1.call-start = ((), (), s32[]{:S(2)}) async-start(), calls=%async_computation.11 | async-start | bytes 6291456 | tf_op jit(solution)/shard_map/psum | solution.py:252
  358.9 246.1 %reduce-scatter.19.cloned.1.call-start = ((), (), s32[]{:S(2)}) async-start(), calls=%async_computation.14 | async-start | bytes 2211840
  372.2 305.4 %reduce-scatter.17.cloned.1.call-start = ((), (), s32[]{:S(2)}) async-start(), calls=%async_computation.13 | async-start | bytes 2654208 | tf_op jit(solution)/shard_map/reduce_scatter | solution.py:279
  378.1 18.7 %copy-start.49 = (f32[768]{0:T(1024)S(1)}, f32[768]{0:T(1024)}, u32[]{:S(2)}) copy-start(f32[768]{0:T(1024)} %get-tuple-element.43) | copy-start | bytes 9220
  378.1 372.3 %reduce-scatter.15.cloned.1.call-start = ((), (), s32[]{:S(2)}) async-start(), calls=%async_computation.12 | async-start | bytes 2654208 | tf_op jit(solution)/shard_map/reduce_scatter | solution.py:278
  382.9 15.9 %copy-start.51 = (f32[768]{0:T(1024)S(1)}, f32[768]{0:T(1024)}, u32[]{:S(2)}) copy-start(f32[768]{0:T(1024)} %get-tuple-element.33) | copy-start | bytes 9220
  382.9 15.9 %copy-start.50 = (f32[768]{0:T(1024)S(1)}, f32[768]{0:T(1024)}, u32[]{:S(2)}) copy-start(f32[768]{0:T(1024)} %get-tuple-element.38) | copy-start | bytes 9220
  382.9 16.0 %copy-start.53 = (f32[768]{0:T(1024)S(1)}, f32[768]{0:T(1024)}, u32[]{:S(2)}) copy-start(f32[768]{0:T(1024)} %get-tuple-element.50) | copy-start | bytes 9220
  382.9 16.0 %copy-start.52 = (f32[768]{0:T(1024)S(1)}, f32[768]{0:T(1024)}, u32[]{:S(2)}) copy-start(f32[768]{0:T(1024)} %get-tuple-element.60) | copy-start | bytes 9220
  382.9 82.0 %copy-start.17 = (f32[512,192]{0,1:T(8,128)S(1)}, f32[512,192]{0,1:T(8,128)}, u32[]{:S(2)}) copy-start(f32[512,192]{0,1:T(8,128)} %reduce-scatter.13.cloned.1.call-done) | copy-start | bytes 1179652
  398.8 137.4 %copy-start.41 = (f32[1024]{0:T(1024)S(1)}, f32[1024]{0:T(1024)}, u32[]{:S(2)}) copy-start(f32[1024]{0:T(1024)} %copy-done.40) | copy-start | bytes 12292
  (57 other events, 217.0 us)
Sparse Core Ops, SparseCore 0:
  94.0 66.6 all-reduce.5
  175.8 68.5 all-reduce.9
  280.7 35.5 reduce-scatter.12
  318.5 34.2 reduce-scatter.10
  355.0 41.6 all-reduce.7
  399.9 63.3 reduce-scatter.20
  465.6 67.4 all-reduce.11
  536.6 68.3 reduce-scatter.18
  609.1 68.4 reduce-scatter.16
  681.5 68.8 reduce-scatter.14
